TPU v7x, 1024 devices: a whole 8x8x8 slice. The times are simulated.
1024 devices in a mesh: section: 64 (over x, y), tensor: 16 (over z, core).
Axes of the slice: x: 8, y: 8, z: 8, core: 2. Of those that a mesh axis runs over, the one named last changes fastest.
Arguments:
- vision_states: bfloat16 [256, 8192], P('section', 'tensor'), may hold values from -6 to 6
- projection: bfloat16 [64, 8192, 2, 2, 128], P('section', 'tensor'), may hold values from -0.0625 to 0.0625
- queries: bfloat16 [64, 2048, 2048], P('section', None, 'tensor'), may hold values from -400 to 400
- cotangent: bfloat16 [64, 2048, 2048], P('section', None, 'tensor'), may hold values from -6 to 6
- gate_logit: float32 [16], replicated, may hold values from 0.3 to 1.5
- tile_counts: int32 [2], replicated, may hold values from 1 to 4, as said below
Outputs:
- attended: bfloat16 [64, 2048, 2048], P('section', None, 'tensor')
- query_grad: bfloat16 [64, 2048, 2048], P('section', None, 'tensor')
- image_grad: float32 [256, 8192], P('section', 'tensor')
Inputs may be any that keep to these rules, and one draw needn't show every extreme that they name: `tile_counts`: some sample has all 4 tiles and some sample has fewer.
All inputs are finite; a program needn't handle non-finite values.
Results may differ from a plain program's by a relative error of at most 0.025.
The roundings to bfloat16 on the way count: a program that leaves them out, or rounds other values in their place, can miss the bound.
Values may be sent and summed in bfloat16 or wider, within the bound.
A program may use at most 32 MiB of HBM per device.

v0:
```python
import jax
import jax.numpy as jnp
from jax import lax
from jax.sharding import PartitionSpec as P

HEAD_DIM = 128
GROUPS = 4
TILE_ROWS = 32


def on_device(vision_states, projection, queries, cotangent, gate_logit, tile_counts):
    whole_image = lax.all_gather(vision_states, "section", axis=0, tiled=True)
    widths = projection.shape[1]
    head_count = projection.shape[2]
    tensor_size = lax.axis_size("tensor")
    local_heads = max(1, head_count // tensor_size)
    repeat_count = max(1, tensor_size // head_count)
    entry_weight = jnp.repeat(projection[0], repeat_count, axis=1).reshape(widths, -1)
    total_rows = whole_image.shape[0]
    summed = lax.psum_scatter(
        lax.dot_general(
            entry_weight, whole_image, (((0,), (1,)), ((), ())), preferred_element_type=jnp.float32
        ),
        "tensor",
        scatter_dimension=0,
        tiled=True,
    )
    key_values = summed.astype(jnp.bfloat16).reshape(local_heads, 2, HEAD_DIM, total_rows)
    samples = tile_counts.shape[0]
    tokens = queries.shape[1]
    sample_tok = tokens // samples
    image_per = total_rows // samples
    head_local = queries.shape[2] // HEAD_DIM
    per_group = head_local // local_heads
    query_heads = queries.reshape(samples, sample_tok, local_heads, per_group, HEAD_DIM)
    keys_cols = key_values[:, 0].reshape(local_heads, HEAD_DIM, samples, image_per)
    values_cols = key_values[:, 1].reshape(local_heads, HEAD_DIM, samples, image_per)
    score_scale = HEAD_DIM ** (-0.5)
    scores = (
        jnp.einsum("bikqd,kdbj->bkqij", query_heads, keys_cols, preferred_element_type=jnp.float32)
        * score_scale
    )
    positions = lax.broadcasted_iota(jnp.int32, (samples, image_per), 1)
    usable = (positions < (tile_counts * TILE_ROWS)[:, None])[:, None, None, None, :]
    masked = jnp.where(usable, scores, -1e30)
    row_max = jnp.max(masked, axis=-1, keepdims=True)
    weights = jnp.where(usable, jnp.exp(masked - row_max), 0.0)
    probabilities = weights / jnp.sum(weights, axis=-1, keepdims=True)
    probs_low = probabilities.astype(jnp.bfloat16)
    layer_index = lax.axis_index("section") // GROUPS
    gate_value = jnp.tanh(lax.dynamic_index_in_dim(gate_logit, layer_index, 0, keepdims=False))
    combined = jnp.einsum(
        "bkqij,kdbj->bikqd", probs_low, values_cols, preferred_element_type=jnp.float32
    )
    attended = (gate_value * combined).astype(jnp.bfloat16).reshape(queries.shape)
    grad_input = (gate_value * cotangent.astype(jnp.float32)).astype(jnp.bfloat16)
    grad_input = grad_input.reshape(samples, sample_tok, local_heads, per_group, HEAD_DIM)
    grad_probs = jnp.einsum(
        "bikqd,kdbj->bkqij", grad_input, values_cols, preferred_element_type=jnp.float32
    )
    center = jnp.sum(probabilities * grad_probs, axis=-1, keepdims=True)
    grad_scores = (probabilities * (grad_probs - center)).astype(jnp.bfloat16)
    query_grad = (
        jnp.einsum("bkqij,kdbj->bikqd", grad_scores, keys_cols, preferred_element_type=jnp.float32)
        * score_scale
    )
    query_grad = query_grad.astype(jnp.bfloat16).reshape(queries.shape)
    key_grad = (
        jnp.einsum(
            "bkqij,bikqd->kdbj", grad_scores, query_heads, preferred_element_type=jnp.float32
        )
        * score_scale
    )
    value_grad = jnp.einsum(
        "bkqij,bikqd->kdbj", probs_low, grad_input, preferred_element_type=jnp.float32
    )
    partial_grad = jnp.stack([key_grad, value_grad], axis=1).astype(jnp.bfloat16)
    partial_grad = partial_grad.reshape(local_heads * 2 * HEAD_DIM, total_rows)
    folded = lax.dot_general(
        lax.all_gather(partial_grad, "tensor", axis=0, tiled=True),
        entry_weight,
        (((0,), (1,)), ((), ())),
        preferred_element_type=jnp.float32,
    )
    image_grad = lax.psum_scatter(folded, "section", scatter_dimension=0, tiled=True)
    return (attended, query_grad, image_grad)


def solution(mesh):
    return jax.shard_map(
        on_device,
        mesh=mesh,
        in_specs=(
            P("section", "tensor"),
            P("section", "tensor", None, None, None),
            P("section", None, "tensor"),
            P("section", None, "tensor"),
            P(),
            P(),
        ),
        out_specs=(
            P("section", None, "tensor"),
            P("section", None, "tensor"),
            P("section", "tensor"),
        ),
        check_vma=False,
    )
```

profile of v0, /device:TPU:1, one launch (start us, length us, event | category | flops | bytes accessed | tf_op | source)
XLA Modules:
  0.0 377.4 jit_solution(4898617601868816359)
XLA Ops:
  7.2 5.2 %broadcast_in_dim.28 = bf16[512,2,8,2,128]{4,3,2,1,0:T(2,128)(2,1)} broadcast(bf16[512,2,2,128]{3,2,1,0:T(2,128)(2,1)} %bitcast.75), dimensions={0,1,3,4} | broadcast | bytes 4718592 | tf_op jit(solution)/shard_map/broadcast_in_dim | solution.py:18
  12.4 7.8 %reshape_reshape.3 = bf16[512,4096]{1,0:T(8,128)(2,1)} reshape(bf16[512,2,8,2,128]{4,3,2,1,0:T(2,128)(2,1)} %broadcast_in_dim.28) | data formatting | bytes 8388608 | tf_op jit(solution)/shard_map/reshape;reshape | solution.py:18
  20.3 39.8 %all-gather = bf16[64,4,512]{2,1,0:T(4,128)(2,1)S(1)} all-gather(bf16[1,4,512]{2,1,0:T(4,128)(2,1)S(1)} %bitcast.85), channel_id=1, replica_groups=mesh['section'=64,'tensor'=16] {'section'}, dimensions={0}, use_global_device_ids=true | all-gather | bytes 266240 | tf_op jit(solution)/shard_map/all_gather | solution.py:12
  60.0 0.1 reshape.124
  60.1 5.5 %fusion.21 = f32[4096,256]{1,0:T(8,128)} fusion(bf16[512,4096]{1,0:T(8,128)(2,1)} %reshape_reshape.3, bf16[256,512]{1,0:T(8,128)(2,1)S(1)} %reshape.124), kind=kOutput, calls=%fused_computation.34 | convolution fusion | flops 1073741824 | bytes 8650752 | tf_op jit(solution)/shard_map/dot_general | solution.py:21
  65.6 0.0 all-gather.3.cloned.1.call-start
  65.6 0.6 copy-done.3
  66.2 0.6 dynamic_slice.4
  67.5 0.1 iota_compare_fusion
  67.6 0.1 multiply_convert_fusion.1
  67.7 84.5 %reduce-scatter.2.cloned.1.call-done = f32[256,256]{1,0:T(8,128)} async-done(((f32[4096,256]{1,0:T(8,128)}), f32[256,256]{1,0:T(8,128)}) %reduce-scatter.2.cloned.1.call-update) | async-done | bytes 262160 | tf_op jit(solution)/shard_map/reduce_scatter | solution.py:20
  152.2 1.0 convert_element_type.40
  153.2 0.1 copy.48
  153.3 0.1 copy.30
  153.4 0.3 fusion.20
  153.7 0.2 fusion.11
  154.0 0.4 fusion.8
  154.4 0.4 multiply_reduce_fusion
  154.8 0.4 fusion.12
  155.1 0.3 fusion.9
  155.5 0.1 copy.40
  155.6 0.7 copy.51
  156.3 0.0 all-reduce.3.cloned.1.call-start
  156.3 47.3 %all-gather.3.cloned.1.call-done = bf16[4096,256]{1,0:T(8,128)(2,1)} async-done(((bf16[256,256]{1,0:T(8,128)(2,1)}), bf16[4096,256]{1,0:T(8,128)(2,1)}) %all-gather.3.cloned.1.call-update) | async-done | bytes 2097168 | tf_op jit(solution)/shard_map/all_gather | solution.py:80
  203.7 4.9 %fusion.22 = f32[256,512]{1,0:T(8,128)} fusion(bf16[4096,256]{1,0:T(8,128)(2,1)} %all-gather.3.cloned.1.call-done, bf16[512,4096]{1,0:T(8,128)(2,1)} %reshape_reshape.3), kind=kOutput, calls=%fused_computation.35 | convolution fusion | flops 1073741824 | bytes 6815744 | tf_op jit(solution)/shard_map/dot_general | solution.py:79
  208.6 1.3 dynamic-slice
  210.5 0.4 fusion.6
  210.9 1.0 copy.33
  211.9 0.3 fusion.5
  212.3 1.0 copy.36
  213.3 156.2 %all-reduce.3.cloned.1.call-done = f32[256,512]{1,0:T(8,128)} async-done(((f32[256,512]{1,0:T(8,128)}), f32[256,512]{1,0:T(8,128)}) %all-reduce.3.cloned.1.call-update) | async-done | bytes 524304
  369.5 1.3 constant_dynamic-slice_fusion
  (16 shorter events, 0.1 us)
Async XLA Ops:
  7.2 146.2 %copy-start = (bf16[1,2048,128]{2,1,0:T(8,128)(2,1)S(1)}, bf16[1,2048,128]{2,1,0:T(8,128)(2,1)}, u32[]{:S(2)}) copy-start(bf16[1,2048,128]{2,1,0:T(8,128)(2,1)} %param.8) | copy-start | bytes 1572868
  7.2 145.0 %reduce-scatter.2.cloned.1.call-start = ((), (), s32[]{:S(2)}) async-start(), calls=%async_computation.1 | async-start | bytes 4456448 | tf_op jit(solution)/shard_map/reduce_scatter | solution.py:20
  12.4 7.8 %copy-start.2 = (bf16[4,512]{1,0:T(4,128)(2,1)S(1)}, bf16[4,512]{1,0:T(4,128)(2,1)}, u32[]{:S(2)}) copy-start(bf16[4,512]{1,0:T(4,128)(2,1)} %param.6) | copy-start | bytes 12292
  65.5 0.7 copy-start.3
  65.5 1.9 copy-start.4
  65.5 2.0 copy-start.1
  65.6 138.1 %all-gather.3.cloned.1.call-start = ((), (), s32[]{:S(2)}) async-start(), calls=%async_computation.2 | async-start | bytes 2228224 | tf_op jit(solution)/shard_map/all_gather | solution.py:80
  156.3 213.2 %all-reduce.3.cloned.1.call-start = ((), (), s32[]{:S(2)}) async-start(), calls=%async_computation.3 | async-start | bytes 1048576
Sparse Core Ops, SparseCore 0:
  65.7 86.4 reduce-scatter.1
  156.4 47.2 all-gather.2
  208.7 160.7 all-reduce.2
where the time goes:
time: 381 us; the launch traced here: 377 us
  waiting for transfers between devices  288 us (76%)
  blocking collectives  39.8 us (10%)
  local copies, waits for them, and re-layouts  19.9 us (5%)
  between operations  15.2 us (4%)
  matrix products  12.5 us (3%)
    unnamed x4, waiting for transfers between devices  156 us
    reduce_scatter x1, waiting for transfers between devices, on_device(): lax.psum_scatter(lax.dot_general(entry_weight, whole_image, (((0,), (1,))...  84.5 us
    all_gather x1, waiting for transfers between devices, on_device(): lax.all_gather(partial_grad, 'tensor', axis=0, tiled=True)  47.3 us
    all_gather x1, blocking collectives, on_device(): whole_image = lax.all_gather(vision_states, 'section', axis=0, tiled=True)  39.8 us
    another operation x1, local copies, waits for them, and re-layouts, on_device(): jnp.repeat(projection[0], repeat_count, axis=1).reshape(widths, -1)  7.8 us
  transfers between devices with their start and end apart: 3, of which 3 were waited for; matrix products, arithmetic and copies ran while one was open for 1% of the time, Pallas kernels for 0%

commit v1 on v0

v1 whole, which is shorter than its diff:
```python
import jax
import jax.numpy as jnp
from jax import lax
from jax.experimental import pallas as pl
from jax.experimental.pallas import tpu as pltpu
from jax.sharding import PartitionSpec as P

MESH = pl.DeviceIdType.MESH
BF16 = jnp.bfloat16
F32 = jnp.float32

HEAD_DIM = 128
GROUPS = 4
TILE_ROWS = 32
TILES = 4
SCALE = HEAD_DIM ** (-0.5)
TOK = 2048
SAMPLE_TOK = 1024
CHUNK = 512
SIDE = 8


def arrived(ref, sem):
    pltpu.make_async_copy(ref, ref, sem).wait()


def kernel(
    vis_ref, w_ref, q_ref, cot_ref, gate_ref, count_ref,
    att_ref, qg_ref, img_ref,
    msg_f, msg, vin, vf, vb, w_raw, w_f, w_cat, w_t,
    q_v, cot_v, gi_v, q_t, gi_t, probs_s, ds_s,
    part, r1, kv, grads, r2, r3, g_f, e_msg, r4, att_v, qg_v,
    load_sem, w_send, w_recv, a_send, a_recv, b1_send, b1_recv, b2_send, b2_recv,
    d1_send, d1_recv, d2_send, d2_recv, e_send, e_recv, out_sem,
):
    sec = lax.axis_index("section")
    ten = lax.axis_index("tensor")
    x, y = sec // SIDE, sec % SIDE
    z, core = ten // 2, ten % 2
    sample = x // 4
    half = z // 4
    tile = z % 4
    slot = ten % 8
    is_own = core == sample

    def tensor_peer(t):
        return (sec, t)

    load_q = pltpu.make_async_copy(q_ref, q_v, load_sem.at[0])
    load_c = pltpu.make_async_copy(cot_ref, cot_v, load_sem.at[1])
    load_w = pltpu.make_async_copy(w_ref, w_raw.at[core], load_sem.at[2])
    load_w.start()
    load_c.start()
    load_q.start()

    barrier = pltpu.get_barrier_semaphore()

    def greet_plane(i, carry):
        tx = 4 * core + (i // 16)
        ty = (i // 2) % SIDE
        m = i % 2
        me = jnp.logical_and(jnp.logical_and(tx == x, ty == y), m == core)

        @pl.when(jnp.logical_not(me))
        def _():
            pl.semaphore_signal(
                barrier, inc=1, device_id=(tx * SIDE + ty, z * 2 + m), device_id_type=MESH
            )

        return carry

    def greet_line(i, carry):
        pl.semaphore_signal(
            barrier, inc=1, device_id=tensor_peer(half * 8 + (slot + i) % 8), device_id_type=MESH
        )
        return carry

    def greet_far(i, carry):
        pl.semaphore_signal(
            barrier, inc=1, device_id=tensor_peer(((1 - half) * 4 + i) * 2 + core),
            device_id_type=MESH,
        )
        return carry

    lax.fori_loop(0, 64, greet_plane, 0)
    lax.fori_loop(1, 8, greet_line, 0)
    lax.fori_loop(0, 4, greet_far, 0)

    for k in range(4):
        msg_f[4 * k : 4 * k + 4, :] = vis_ref[:, 128 * k : 128 * (k + 1)].astype(F32)
    msg[...] = msg_f[...].astype(BF16)

    pl.semaphore_wait(barrier, 75 - is_own.astype(jnp.int32))

    a_slot = (x % 4) * 16 + y * 2 + core

    def a_copy(i):
        tx = (x + 4 + i // SIDE) % SIDE
        ty = (y + 4 + i % SIDE) % SIDE
        me = jnp.logical_and(jnp.logical_and(tx == x, ty == y), is_own)
        return me, pltpu.make_async_remote_copy(
            src_ref=msg, dst_ref=vin.at[a_slot], send_sem=a_send, recv_sem=a_recv.at[x % 4],
            device_id=(tx * SIDE + ty, z * 2 + sample), device_id_type=MESH,
        )

    def a_start(i, carry):
        me, copy = a_copy(i)

        @pl.when(me)
        def _():
            pltpu.make_async_copy(msg, vin.at[a_slot], a_recv.at[x % 4]).start()

        @pl.when(jnp.logical_not(me))
        def _():
            copy.start()

        return carry

    lax.fori_loop(0, 64, a_start, 0)
    w_copy = pltpu.make_async_remote_copy(
        src_ref=w_ref, dst_ref=w_raw.at[core], send_sem=w_send, recv_sem=w_recv,
        device_id=tensor_peer(z * 2 + 1 - core), device_id_type=MESH,
    )
    w_copy.start()

    gate = jnp.tanh(jnp.full((8, 128), gate_ref[sec // GROUPS], F32))[0:1, 0:1]

    def lay_out(m):
        w_f[...] = w_raw[m].astype(F32)
        for n in range(4):
            block = w_f[pl.ds(n, 512, stride=4), :]
            w_cat[m, :, 128 * n : 128 * (n + 1)] = block.astype(BF16)
            w_t[m, 128 * n : 128 * (n + 1), :] = block.T.astype(BF16)

    load_w.wait()
    lay_out(core)
    w_copy.wait_recv()
    lay_out(1 - core)
    load_c.wait()
    load_q.wait()
    for t in range(TOK // CHUNK):
        rows = slice(t * CHUNK, (t + 1) * CHUNK)
        gi = (gate * cot_v[rows, :].astype(F32)).astype(BF16)
        gi_v[rows, :] = gi
        gi_t[:, rows] = gi.astype(F32).T.astype(BF16)
        q_t[:, rows] = q_v[rows, :].astype(F32).T.astype(BF16)

    def b1_copy(dest, source):
        return pltpu.make_async_remote_copy(
            src_ref=part.at[dest], dst_ref=r1.at[z], send_sem=b1_send, recv_sem=b1_recv,
            device_id=tensor_peer(dest * 2 + core), device_id_type=MESH,
        )

    for j in range(TILES):
        arrived(vin.at[pl.ds(16 * j, 16)], a_recv.at[j])
        vf[...] = vin[16 * j : 16 * (j + 1)].reshape(256, 128).astype(F32)
        for m in range(2):
            for k in range(4):
                rows = [vf[pl.ds(m * 16 + 4 * k + r, 8, stride=32), :] for r in range(4)]
                vb[m, :, 128 * k : 128 * (k + 1)] = jnp.concatenate(rows, axis=0).astype(BF16)
        total = jnp.dot(vb[0], w_cat[0], preferred_element_type=F32) + jnp.dot(
            vb[1], w_cat[1], preferred_element_type=F32
        )
        for g in range(2):
            dest = 4 * g + j
            part[dest] = total[:, 256 * g : 256 * (g + 1)]

            @pl.when(dest != z)
            def _():
                b1_copy(dest, j).start()

    arrived(r1.at[pl.ds(0, 7)], b1_recv)
    total = part[z]
    for i in range(1, 8):
        total = total + r1[(z + i) % 8]
    kv_slot = core * 4 + tile
    kv[kv_slot] = total.astype(BF16)

    def b2_start(i, carry):
        pltpu.make_async_remote_copy(
            src_ref=kv.at[kv_slot], dst_ref=kv.at[kv_slot], send_sem=b2_send, recv_sem=b2_recv,
            device_id=tensor_peer(half * 8 + (slot + i) % 8), device_id_type=MESH,
        ).start()
        return carry

    lax.fori_loop(1, 8, b2_start, 0)
    arrived(kv.at[pl.ds(0, 7)], b2_recv)

    row_tile = lax.broadcasted_iota(jnp.int32, (128, CHUNK), 0) // TILE_ROWS
    for b in range(2):
        both = kv[4 * b : 4 * b + 4].reshape(128, 256)
        keys, values = both[:, :128], both[:, 128:]
        usable = row_tile < count_ref[b]
        key_grad = jnp.zeros((128, HEAD_DIM), F32)
        value_grad = jnp.zeros((128, HEAD_DIM), F32)
        for t in range(SAMPLE_TOK // CHUNK):
            rows = slice(b * SAMPLE_TOK + t * CHUNK, b * SAMPLE_TOK + (t + 1) * CHUNK)
            scores = jnp.dot(keys, q_t[:, rows], preferred_element_type=F32) * SCALE
            masked = jnp.where(usable, scores, -1e30)
            row_max = jnp.max(masked, axis=0, keepdims=True)
            weights = jnp.where(usable, jnp.exp(masked - row_max), 0.0)
            probs = weights * (1.0 / jnp.sum(weights, axis=0, keepdims=True))
            probs_low = probs.astype(BF16)
            grad_probs = jnp.dot(values, gi_t[:, rows], preferred_element_type=F32)
            center = jnp.sum(probs * grad_probs, axis=0, keepdims=True)
            grad_scores = (probs * (grad_probs - center)).astype(BF16)
            key_grad = key_grad + jnp.dot(grad_scores, q_v[rows, :], preferred_element_type=F32)
            value_grad = value_grad + jnp.dot(probs_low, gi_v[rows, :], preferred_element_type=F32)
            probs_s[:, rows] = probs_low
            ds_s[:, rows] = grad_scores
        part_grads = jnp.concatenate([(key_grad * SCALE).astype(BF16), value_grad.astype(BF16)], axis=1)
        grads[4 * b : 4 * b + 4] = part_grads.reshape(4, 32, 256)

        for j in range(TILES):
            dest = j * 2 + b

            @pl.when(dest != slot)
            def _():
                pltpu.make_async_remote_copy(
                    src_ref=grads.at[4 * b + j], dst_ref=r2.at[slot],
                    send_sem=d1_send, recv_sem=d1_recv,
                    device_id=tensor_peer(half * 8 + dest), device_id_type=MESH,
                ).start()

    def outputs(b):
        both = kv[4 * b : 4 * b + 4].reshape(128, 256).astype(F32)
        keys_t, values_t = both[:, :128].T.astype(BF16), both[:, 128:].T.astype(BF16)
        for t in range(SAMPLE_TOK // CHUNK):
            rows = slice(b * SAMPLE_TOK + t * CHUNK, b * SAMPLE_TOK + (t + 1) * CHUNK)
            combined = jnp.dot(values_t, probs_s[:, rows], preferred_element_type=F32)
            att_v[rows, :] = (gate * combined).T.astype(BF16)
            query_grad = jnp.dot(keys_t, ds_s[:, rows], preferred_element_type=F32) * SCALE
            qg_v[rows, :] = query_grad.T.astype(BF16)

    outputs(0)
    arrived(r2.at[pl.ds(0, 7)], d1_recv)
    total = grads[kv_slot].astype(F32)
    for i in range(1, 8):
        total = total + r2[(slot + i) % 8].astype(F32)
    r3[z] = total.astype(BF16)

    def d2_start(i, carry):
        pltpu.make_async_remote_copy(
            src_ref=r3.at[z], dst_ref=r3.at[z], send_sem=d2_send, recv_sem=d2_recv,
            device_id=tensor_peer(((z + i) % 8) * 2 + core), device_id_type=MESH,
        ).start()
        return carry

    lax.fori_loop(1, 8, d2_start, 0)
    outputs(1)
    store_a = pltpu.make_async_copy(att_v, att_ref, out_sem.at[0])
    store_q = pltpu.make_async_copy(qg_v, qg_ref, out_sem.at[1])
    store_a.start()
    store_q.start()
    arrived(r3.at[pl.ds(0, 7)], d2_recv)

    sums = jnp.concatenate([r3[0:4].reshape(128, 256), r3[4:8].reshape(128, 256)], axis=1)
    for m in range(2):
        grad = jnp.dot(sums, w_t[m], preferred_element_type=F32)
        for j in range(TILES):
            for k in range(4):
                for r in range(4):
                    g_f[pl.ds(256 * j + 16 * m + 4 * k + r, 8, stride=32), :] = grad[
                        32 * j + 8 * r : 32 * j + 8 * (r + 1), 128 * k : 128 * (k + 1)
                    ]
    e_msg[...] = g_f[...].astype(BF16).reshape(64, 16, 128)

    def e_start(i, carry):
        j = (x + 2 + i // 16) % 4
        ty = (y + 4 + (i // 2) % SIDE) % SIDE
        m = i % 2
        tx = 4 * core + j
        source = e_msg.at[j * 16 + ty * 2 + m]
        me = jnp.logical_and(jnp.logical_and(tx == x, ty == y), m == core)

        @pl.when(me)
        def _():
            pltpu.make_async_copy(source, r4.at[sec], e_recv).start()

        @pl.when(jnp.logical_not(me))
        def _():
            pltpu.make_async_remote_copy(
                src_ref=source, dst_ref=r4.at[sec], send_sem=e_send, recv_sem=e_recv,
                device_id=(tx * SIDE + ty, z * 2 + m), device_id_type=MESH,
            ).start()

        return carry

    lax.fori_loop(0, 64, e_start, 0)

    w_copy.wait_send()
    arrived(part.at[pl.ds(0, 7)], b1_send)
    arrived(kv.at[pl.ds(0, 7)], b2_send)
    arrived(grads.at[pl.ds(0, 7)], d1_send)
    arrived(r3.at[pl.ds(0, 7)], d2_send)

    @pl.when(is_own)
    def _():
        arrived(vin.at[pl.ds(0, 63)], a_send)
        arrived(e_msg.at[pl.ds(0, 63)], e_send)

    @pl.when(jnp.logical_not(is_own))
    def _():
        arrived(vin, a_send)
        arrived(e_msg, e_send)

    arrived(r4, e_recv)
    image = jnp.sum(r4[...].astype(F32), axis=0)
    for k in range(4):
        img_ref[:, 128 * k : 128 * (k + 1)] = image[4 * k : 4 * k + 4, :]
    store_a.wait()
    store_q.wait()


def on_device(vision_states, projection, queries, cotangent, gate_logit, tile_counts):
    vmem = pl.BlockSpec(memory_space=pltpu.VMEM)
    smem = pl.BlockSpec(memory_space=pltpu.SMEM)
    hbm = pl.BlockSpec(memory_space=pl.ANY)
    dma = pltpu.SemaphoreType.DMA
    tile8 = pltpu.VMEM((8, 32, 256), BF16)
    tok = pltpu.VMEM((TOK, HEAD_DIM), BF16)
    tok_t = pltpu.VMEM((HEAD_DIM, TOK), BF16)
    blocks = pltpu.VMEM((64, 16, 128), BF16)
    attended, query_grad, image_grad = pl.pallas_call(
        kernel,
        out_shape=(
            jax.ShapeDtypeStruct((TOK, HEAD_DIM), BF16),
            jax.ShapeDtypeStruct((TOK, HEAD_DIM), BF16),
            jax.ShapeDtypeStruct((4, 512), F32),
        ),
        in_specs=[vmem, hbm, hbm, hbm, smem, smem],
        out_specs=(hbm, hbm, vmem),
        scratch_shapes=[
            pltpu.VMEM((16, 128), F32),
            pltpu.VMEM((16, 128), BF16),
            blocks,
            pltpu.VMEM((256, 128), F32),
            pltpu.VMEM((2, 32, 512), BF16),
            pltpu.VMEM((2, 2048, 128), BF16),
            pltpu.VMEM((2048, 128), F32),
            pltpu.VMEM((2, 512, 512), BF16),
            pltpu.VMEM((2, 512, 512), BF16),
            tok, tok, tok, tok_t, tok_t, tok_t, tok_t,
            pltpu.VMEM((8, 32, 256), F32),
            pltpu.VMEM((8, 32, 256), F32),
            tile8, tile8, tile8, tile8,
            pltpu.VMEM((1024, 128), F32),
            blocks, blocks,
            tok, tok,
            dma((3,)), dma, dma, dma, dma((4,)), dma, dma, dma, dma,
            dma, dma, dma, dma, dma, dma, dma((2,)),
        ],
        compiler_params=pltpu.CompilerParams(collective_id=0, has_side_effects=True),
        name="cross_attention",
    )(
        vision_states,
        projection.reshape(2048, 128),
        queries.reshape(TOK, HEAD_DIM),
        cotangent.reshape(TOK, HEAD_DIM),
        gate_logit,
        tile_counts,
    )
    return (
        attended.reshape(queries.shape),
        query_grad.reshape(queries.shape),
        image_grad,
    )


def solution(mesh):
    return jax.shard_map(
        on_device,
        mesh=mesh,
        in_specs=(
            P("section", "tensor"),
            P("section", "tensor", None, None, None),
            P("section", None, "tensor"),
            P("section", None, "tensor"),
            P(),
            P(),
        ),
        out_specs=(
            P("section", None, "tensor"),
            P("section", None, "tensor"),
            P("section", "tensor"),
        ),
        check_vma=False,
    )
```

time: 381 us -> 74.6 us (0.20)
  waiting for transfers between devices: 288 us -> 0 us
  Pallas kernels: 0 us -> 70.4 us
  blocking collectives: 39.8 us -> 0 us
  local copies, waits for them, and re-layouts: 19.9 us -> 3.33 us
  between operations: 15.2 us -> 0.65 us
  matrix products: 12.5 us -> 0 us
    unnamed x4 -> x0, waiting for transfers between devices: 156 us -> none
    reduce_scatter x1 -> x0, waiting for transfers between devices: 84.5 us -> none  [on_device(): lax.psum_scatter(lax.dot_general(entry_weight, whole_image, (((0,), (1,))...]
    pallas_call x0 -> x1, Pallas kernels: none -> 70.4 us  [on_device(): pl.pallas_call(kernel, out_shape=(jax.ShapeDtypeStruct((TOK, HEAD_DIM), B...]
    all_gather x1 -> x0, waiting for transfers between devices: 47.3 us -> none  [on_device(): lax.all_gather(partial_grad, 'tensor', axis=0, tiled=True)]
    all_gather x1 -> x0, blocking collectives: 39.8 us -> none  [on_device(): whole_image = lax.all_gather(vision_states, 'section', axis=0, tiled=True)]
    dot_general x8 -> x0, matrix products: 12.5 us -> none  [the longest x1 5.47 us: on_device(): lax.dot_general(entry_weight, whole_image, (((0,), (1,)), ((), ())), pref...]
    another operation x2 -> x0, local copies, waits for them, and re-layouts: 7.93 us -> none  [the longest x1 7.8 us: on_device(): jnp.repeat(projection[0], repeat_count, axis=1).reshape(widths, -1)]
    broadcast_in_dim x1 -> x0, local copies, waits for them, and re-layouts: 5.22 us -> none  [on_device(): jnp.repeat(projection[0], repeat_count, axis=1).reshape(widths, -1)]
  transfers between devices with their start and end apart: 3 -> 0, of which waited for: 3 -> 0; matrix products, arithmetic and copies ran while one was open for 1% -> 0% of each run, Pallas kernels for 0% -> 0%
where the time goes in v1:
time: 74.6 us; the launch traced here: 74.4 us
  Pallas kernels  70.4 us (94%)
  local copies, waits for them, and re-layouts  3.33 us (4%)
    pallas_call x1, Pallas kernels, on_device(): pl.pallas_call(kernel, out_shape=(jax.ShapeDtypeStruct((TOK, HEAD_DIM), B...  70.4 us
    unnamed x7, local copies, waits for them, and re-layouts  3.33 us

profile of v1, /device:TPU:1, one launch (start us, length us, event | category | flops | bytes accessed | tf_op | source)
XLA Modules:
  0.0 74.4 jit_solution(7333218489820851012)
XLA Ops:
  0.6 70.4 %cross_attention.1 = (bf16[2048,128]{1,0:T(8,128)(2,1)}, bf16[2048,128]{1,0:T(8,128)(2,1)}, f32[4,512]{1,0:T(4,128)}) custom-call(bf16[4,512]{1,0:T(4,128)(2,1)} %vis_ref.1, bf16[2048,128]{1,0:T(8,128)(2,1)} %bitcast.7, bf16[2048,128]{1,0:T(8,128)(2,1)} %bitcast.8, bf16[2048,128]{1,0:T(8,128)(2,1)} %bitcast.9, f32[16]{0:T(128)} %gate_ref.1, s32[2]{0:T(128)} %count_ref.1), custom_call_target="tpu_custom_call" | custom-call | tf_op jit(solution)/shard_map/cross_attention/pallas_call | solution.py:324
  71.0 0.0 copy-start
  71.1 1.9 %copy.12 = bf16[1,2048,128]{2,1,0:T(8,128)(2,1)} copy(bf16[1,2048,128]{2,1,0:T(8,128)(2,1)} %bitcast.6) | data formatting | bytes 1048576
  73.0 0.0 copy-done
  73.0 0.0 copy-start.1
  73.0 0.8 %copy.13 = bf16[1,2048,128]{2,1,0:T(8,128)(2,1)} copy(bf16[1,2048,128]{2,1,0:T(8,128)(2,1)S(1)} %bitcast.5) | data formatting | bytes 1048576
  73.8 0.0 copy-done.1
  73.8 0.6 copy.14
Async XLA Ops:
  71.0 1.9 %copy-start = (bf16[2048,128]{1,0:T(8,128)(2,1)S(1)}, bf16[2048,128]{1,0:T(8,128)(2,1)}, u32[]{:S(2)}) copy-start(bf16[2048,128]{1,0:T(8,128)(2,1)} %get-tuple-element.7) | copy-start | bytes 1572868
  73.0 0.8 %copy-start.1 = (f32[4,512]{1,0:T(4,128)S(1)}, f32[4,512]{1,0:T(4,128)}, u32[]{:S(2)}) copy-start(f32[4,512]{1,0:T(4,128)} %get-tuple-element.14) | copy-start | bytes 24580

commit v2 on v1

v2 whole, which is shorter than its diff:
```python
import jax
import jax.numpy as jnp
from jax import lax
from jax.experimental import pallas as pl
from jax.experimental.pallas import tpu as pltpu
from jax.sharding import PartitionSpec as P

MESH = pl.DeviceIdType.MESH
BF16 = jnp.bfloat16
F32 = jnp.float32

HEAD_DIM = 128
GROUPS = 4
TILE_ROWS = 32
TILES = 4
SCALE = HEAD_DIM ** (-0.5)
TOK = 2048
SAMPLE_TOK = 1024
CHUNK = 512
SIDE = 8
FAR_FIRST = (4, 3, 5, 2, 6, 1, 7)


def arrived(ref, sem):
    pltpu.make_async_copy(ref, ref, sem).wait()


def kernel(
    vis_ref, w_ref, q_ref, cot_ref, gate_ref, count_ref,
    att_ref, qg_ref, img_ref,
    gate_s, count_s, vis_v, msg_f, msg, vin_a, vin_b, vf, vb_a, vb_b, w_raw, w_f, w_cat, w_t,
    q_v, cot_v, gi_v, q_t, gi_t, probs_s, ds_s,
    part, r1, kv, grads, r2, r3, g_f, em_a, em_b, ea1, eb1, es_a, es_b, e2,
    load_sem, w_send, w_recv, a1_send, a1a_recv, a1b_recv, a2a_send, a2b_send, a2a_recv, a2b_recv,
    b1_send, b1_recv, b2_send, b2_recv, d1_send, d1_recv, d2_send, d2_recv,
    ea1_send, eb1_send, ea1_recv, eb1_recv, e2a_send, e2b_send, e2_recv,
):
    sec = lax.axis_index("section")
    ten = lax.axis_index("tensor")
    x, y = sec // SIDE, sec % SIDE
    z, core = ten // 2, ten % 2
    sample = x // 4
    half = z // 4
    tile = x % 4
    sum_tile = z % 4
    slot = ten % 8
    is_own = core == sample

    def chip(cx, cy, c):
        return (cx * SIDE + cy, z * 2 + c)

    def tensor_peer(t):
        return (sec, t)

    def remote(src, dst, send, recv, device):
        return pltpu.make_async_remote_copy(
            src_ref=src, dst_ref=dst, send_sem=send, recv_sem=recv,
            device_id=device, device_id_type=MESH,
        )

    load_v = pltpu.make_async_copy(vis_ref, vis_v, load_sem.at[3])
    load_q = pltpu.make_async_copy(q_ref, q_v, load_sem.at[0])
    load_c = pltpu.make_async_copy(cot_ref, cot_v, load_sem.at[1])
    load_w = pltpu.make_async_copy(w_ref, w_raw.at[core], load_sem.at[2])
    load_g = pltpu.make_async_copy(gate_ref, gate_s, load_sem.at[4])
    load_n = pltpu.make_async_copy(count_ref, count_s, load_sem.at[5])
    load_v.start()
    load_g.start()
    load_n.start()
    load_w.start()
    load_c.start()
    load_q.start()

    barrier = pltpu.get_barrier_semaphore()

    def greet(device):
        pl.semaphore_signal(barrier, inc=1, device_id=device, device_id_type=MESH)

    for d in FAR_FIRST:
        for c in range(2):
            greet(chip((x + d) % SIDE, y, c))
            greet(chip(x, (y + d) % SIDE, c))
    for i in range(1, 8):
        greet(tensor_peer(half * 8 + (slot + i) % 8))
    for i in range(4):
        greet(tensor_peer(((1 - half) * 4 + i) * 2 + core))

    load_v.wait()
    for k in range(4):
        msg_f[4 * k : 4 * k + 4, :] = vis_v[:, 128 * k : 128 * (k + 1)].astype(F32)
    msg[...] = msg_f[...].astype(BF16)

    pl.semaphore_wait(barrier, 39)

    @pl.when(core == 0)
    def _():
        for d in FAR_FIRST:
            remote(msg, vin_a.at[tile, y], a1_send, a1a_recv, chip(x, (y + d) % SIDE, sample)).start()

        @pl.when(is_own)
        def _():
            pltpu.make_async_copy(msg, vin_a.at[tile, y], a1a_recv).start()

        @pl.when(jnp.logical_not(is_own))
        def _():
            remote(msg, vin_a.at[tile, y], a1_send, a1a_recv, chip(x, y, 1)).start()

    @pl.when(core == 1)
    def _():
        for d in FAR_FIRST:
            remote(msg, vin_b.at[y, tile], a1_send, a1b_recv, chip((x + d) % SIDE, y, sample)).start()

        @pl.when(is_own)
        def _():
            pltpu.make_async_copy(msg, vin_b.at[y, tile], a1b_recv).start()

        @pl.when(jnp.logical_not(is_own))
        def _():
            remote(msg, vin_b.at[y, tile], a1_send, a1b_recv, chip(x, y, 0)).start()

    w_copy = remote(w_ref, w_raw.at[core], w_send, w_recv, tensor_peer(z * 2 + 1 - core))
    w_copy.start()

    def lay_out(m):
        w_f[...] = w_raw[m].astype(F32)
        for n in range(4):
            block = w_f[pl.ds(n, 512, stride=4), :]
            w_cat[m, :, 128 * n : 128 * (n + 1)] = block.astype(BF16)
            w_t[m, 128 * n : 128 * (n + 1), :] = block.T.astype(BF16)

    load_w.wait()
    lay_out(core)

    arrived(vin_b.at[y], a1b_recv)
    for d in FAR_FIRST:
        remote(vin_b.at[y], vin_b.at[y], a2b_send, a2b_recv, chip(x, (y + d) % SIDE, core)).start()

    @pl.when(is_own)
    def _():
        arrived(vin_a.at[tile], a1a_recv)
        for d in FAR_FIRST:
            remote(vin_a.at[tile], vin_a.at[tile], a2a_send, a2a_recv, chip((x + d) % SIDE, y, core)).start()

    load_g.wait()
    load_n.wait()
    gate = jnp.tanh(jnp.full((8, 128), gate_s[sec // GROUPS], F32))[0:1, 0:1]
    w_copy.wait_recv()
    lay_out(1 - core)
    load_c.wait()
    load_q.wait()
    for t in range(TOK // CHUNK):
        rows = slice(t * CHUNK, (t + 1) * CHUNK)
        gi = (gate * cot_v[rows, :].astype(F32)).astype(BF16)
        gi_v[rows, :] = gi
        gi_t[:, rows] = gi.astype(F32).T.astype(BF16)
        q_t[:, rows] = q_v[rows, :].astype(F32).T.astype(BF16)

    def rows_of(blocks, out):
        for j in range(TILES):
            vf[...] = blocks(j).reshape(128, 128).astype(F32)
            for k in range(4):
                rows = [vf[pl.ds(4 * k + r, 8, stride=16), :] for r in range(4)]
                out[32 * j : 32 * (j + 1), 128 * k : 128 * (k + 1)] = jnp.concatenate(
                    rows, axis=0
                ).astype(BF16)

    arrived(vin_b.at[pl.ds(0, 7)], a2b_recv)
    rows_of(lambda j: vin_b[:, j], vb_b)

    @pl.when(is_own)
    def _():
        arrived(vin_a.at[pl.ds(0, 3)], a2a_recv)

    @pl.when(jnp.logical_not(is_own))
    def _():
        arrived(vin_a, a2a_recv)

    rows_of(lambda j: vin_a[j], vb_a)
    total = jnp.dot(vb_a[...], w_cat[0], preferred_element_type=F32) + jnp.dot(
        vb_b[...], w_cat[1], preferred_element_type=F32
    )
    for g in range(2):
        part[4 * g : 4 * g + 4] = total[:, 256 * g : 256 * (g + 1)].reshape(4, 32, 256)
    for d in FAR_FIRST:
        dest = (z + d) % 8
        remote(part.at[dest], r1.at[z], b1_send, b1_recv, tensor_peer(dest * 2 + core)).start()

    arrived(r1.at[pl.ds(0, 7)], b1_recv)
    total = part[z]
    for i in range(1, 8):
        total = total + r1[(z + i) % 8]
    kv_slot = core * 4 + sum_tile
    kv[kv_slot] = total.astype(BF16)

    for i in range(1, 8):
        remote(
            kv.at[kv_slot], kv.at[kv_slot], b2_send, b2_recv,
            tensor_peer(half * 8 + (slot + i) % 8),
        ).start()
    arrived(kv.at[pl.ds(0, 7)], b2_recv)

    row_tile = lax.broadcasted_iota(jnp.int32, (128, CHUNK), 0) // TILE_ROWS
    for b in range(2):
        both = kv[4 * b : 4 * b + 4].reshape(128, 256)
        keys, values = both[:, :128], both[:, 128:]
        usable = row_tile < count_s[b]
        key_grad = jnp.zeros((128, HEAD_DIM), F32)
        value_grad = jnp.zeros((128, HEAD_DIM), F32)
        for t in range(SAMPLE_TOK // CHUNK):
            rows = slice(b * SAMPLE_TOK + t * CHUNK, b * SAMPLE_TOK + (t + 1) * CHUNK)
            scores = jnp.dot(keys, q_t[:, rows], preferred_element_type=F32) * SCALE
            masked = jnp.where(usable, scores, -1e30)
            row_max = jnp.max(masked, axis=0, keepdims=True)
            weights = jnp.where(usable, jnp.exp(masked - row_max), 0.0)
            probs = weights * (1.0 / jnp.sum(weights, axis=0, keepdims=True))
            probs_low = probs.astype(BF16)
            grad_probs = jnp.dot(values, gi_t[:, rows], preferred_element_type=F32)
            center = jnp.sum(probs * grad_probs, axis=0, keepdims=True)
            grad_scores = (probs * (grad_probs - center)).astype(BF16)
            key_grad = key_grad + jnp.dot(grad_scores, q_v[rows, :], preferred_element_type=F32)
            value_grad = value_grad + jnp.dot(probs_low, gi_v[rows, :], preferred_element_type=F32)
            probs_s[:, rows] = probs_low
            ds_s[:, rows] = grad_scores
        part_grads = jnp.concatenate([(key_grad * SCALE).astype(BF16), value_grad.astype(BF16)], axis=1)
        grads[4 * b : 4 * b + 4] = part_grads.reshape(4, 32, 256)

        for j in range(TILES):
            dest = j * 2 + b

            @pl.when(dest != slot)
            def _():
                remote(
                    grads.at[4 * b + j], r2.at[slot], d1_send, d1_recv, tensor_peer(half * 8 + dest)
                ).start()

    def outputs(b):
        both = kv[4 * b : 4 * b + 4].reshape(128, 256).astype(F32)
        keys_t, values_t = both[:, :128].T.astype(BF16), both[:, 128:].T.astype(BF16)
        for t in range(SAMPLE_TOK // CHUNK):
            rows = slice(b * SAMPLE_TOK + t * CHUNK, b * SAMPLE_TOK + (t + 1) * CHUNK)
            combined = jnp.dot(values_t, probs_s[:, rows], preferred_element_type=F32)
            att_ref[rows, :] = (gate * combined).T.astype(BF16)
            query_grad = jnp.dot(keys_t, ds_s[:, rows], preferred_element_type=F32) * SCALE
            qg_ref[rows, :] = query_grad.T.astype(BF16)

    outputs(0)
    arrived(r2.at[pl.ds(0, 7)], d1_recv)
    total = grads[kv_slot].astype(F32)
    for i in range(1, 8):
        total = total + r2[(slot + i) % 8].astype(F32)
    r3[z] = total.astype(BF16)

    for d in FAR_FIRST:
        remote(
            r3.at[z], r3.at[z], d2_send, d2_recv, tensor_peer(((z + d) % 8) * 2 + core)
        ).start()
    outputs(1)
    arrived(r3.at[pl.ds(0, 7)], d2_recv)

    sums = jnp.concatenate([r3[0:4].reshape(128, 256), r3[4:8].reshape(128, 256)], axis=1)

    def spread(m, where, step):
        grad = jnp.dot(sums, w_t[m], preferred_element_type=F32)
        for j in range(TILES):
            for k in range(4):
                for r in range(4):
                    g_f[m, pl.ds(where(j) + 4 * k + r, 8, stride=step), :] = grad[
                        32 * j + 8 * r : 32 * j + 8 * (r + 1), 128 * k : 128 * (k + 1)
                    ]
        return g_f[m].astype(BF16)

    em_b[...] = spread(1, lambda j: 16 * j, 64).reshape(8, 4, 16, 128)
    for d in FAR_FIRST:
        ty = (y + d) % SIDE
        remote(em_b.at[ty], eb1.at[y], eb1_send, eb1_recv, chip(x, ty, core)).start()
    em_a[...] = spread(0, lambda j: 128 * j, 16).reshape(4, 8, 16, 128)
    own_a = jnp.logical_and(core == 0, is_own)
    own_b = jnp.logical_and(core == 1, is_own)
    for i in range(4):
        j = (tile + 2 + i) % 4
        me = jnp.logical_and(own_a, j == tile)

        @pl.when(me)
        def _():
            pltpu.make_async_copy(em_a.at[j], ea1.at[x], ea1_recv).start()

        @pl.when(jnp.logical_not(me))
        def _():
            remote(em_a.at[j], ea1.at[x], ea1_send, ea1_recv, chip(4 * core + j, y, 0)).start()

    arrived(eb1.at[pl.ds(0, 7)], eb1_recv)
    total = em_b[y].astype(F32)
    for d in range(1, 8):
        total = total + eb1[(y + d) % 8].astype(F32)
    es_b[...] = total.astype(BF16)
    for i in range(4):
        j = (tile + 2 + i) % 4
        me = jnp.logical_and(own_b, j == tile)

        @pl.when(me)
        def _():
            pltpu.make_async_copy(es_b.at[j], e2.at[x], e2_recv).start()

        @pl.when(jnp.logical_not(me))
        def _():
            remote(es_b.at[j], e2.at[x], e2b_send, e2_recv, chip(4 * core + j, y, 1)).start()

    @pl.when(core == 0)
    def _():
        arrived(ea1, ea1_recv)
        total = ea1[0].astype(F32)
        for i in range(1, 8):
            total = total + ea1[i].astype(F32)
        es_a[...] = total.astype(BF16)
        for d in FAR_FIRST:
            ty = (y + d) % SIDE
            remote(es_a.at[ty], e2.at[y], e2a_send, e2_recv, chip(x, ty, 0)).start()
        e2[y] = es_a[y]

    w_copy.wait_send()
    arrived(vin_b.at[pl.ds(0, 7)], a2b_send)
    arrived(part.at[pl.ds(0, 7)], b1_send)
    arrived(kv.at[pl.ds(0, 7)], b2_send)
    arrived(grads.at[pl.ds(0, 7)], d1_send)
    arrived(r3.at[pl.ds(0, 7)], d2_send)
    arrived(em_b.at[pl.ds(0, 7)], eb1_send)

    @pl.when(is_own)
    def _():
        arrived(vin_a.at[0, pl.ds(0, 7)], a1_send)
        arrived(ea1.at[pl.ds(0, 7)], a2a_send)

    @pl.when(jnp.logical_not(is_own))
    def _():
        arrived(vin_a.at[0], a1_send)

    @pl.when(own_a)
    def _():
        arrived(em_a.at[pl.ds(0, 3)], ea1_send)

    @pl.when(jnp.logical_not(own_a))
    def _():
        arrived(em_a, ea1_send)

    @pl.when(own_b)
    def _():
        arrived(es_b.at[pl.ds(0, 3)], e2b_send)

    @pl.when(jnp.logical_not(own_b))
    def _():
        arrived(es_b, e2b_send)

    @pl.when(core == 0)
    def _():
        arrived(es_a.at[pl.ds(0, 7)], e2a_send)

    @pl.when(core == 0)
    def _():
        arrived(e2.at[pl.ds(0, 7)], e2_recv)

    @pl.when(core == 1)
    def _():
        arrived(e2, e2_recv)

    image = jnp.sum(e2[...].astype(F32), axis=0)
    for k in range(4):
        img_ref[:, 128 * k : 128 * (k + 1)] = image[4 * k : 4 * k + 4, :]


def on_device(vision_states, projection, queries, cotangent, gate_logit, tile_counts):
    vmem = pl.BlockSpec(memory_space=pltpu.VMEM)
    hbm = pl.BlockSpec(memory_space=pltpu.HBM)
    dma = pltpu.SemaphoreType.DMA
    tile8 = pltpu.VMEM((8, 32, 256), BF16)
    tok = pltpu.VMEM((TOK, HEAD_DIM), BF16)
    tok_t = pltpu.VMEM((HEAD_DIM, TOK), BF16)

    def blocks(*lead):
        return pltpu.VMEM((*lead, 16, 128), BF16)

    attended, query_grad, image_grad = pl.pallas_call(
        kernel,
        out_shape=(
            jax.ShapeDtypeStruct((TOK, HEAD_DIM), BF16),
            jax.ShapeDtypeStruct((TOK, HEAD_DIM), BF16),
            jax.ShapeDtypeStruct((4, 512), F32),
        ),
        in_specs=[hbm] * 6,
        out_specs=(vmem, vmem, vmem),
        scratch_shapes=[
            pltpu.SMEM((16,), F32),
            pltpu.SMEM((2,), jnp.int32),
            pltpu.VMEM((4, 512), BF16),
            pltpu.VMEM((16, 128), F32),
            blocks(),
            blocks(4, 8), blocks(8, 4),
            pltpu.VMEM((128, 128), F32),
            pltpu.VMEM((128, 512), BF16),
            pltpu.VMEM((128, 512), BF16),
            pltpu.VMEM((2, 2048, 128), BF16),
            pltpu.VMEM((2048, 128), F32),
            pltpu.VMEM((2, 512, 512), BF16),
            pltpu.VMEM((2, 512, 512), BF16),
            tok, tok, tok, tok_t, tok_t, tok_t, tok_t,
            pltpu.VMEM((8, 32, 256), F32),
            pltpu.VMEM((8, 32, 256), F32),
            tile8, tile8, tile8, tile8,
            pltpu.VMEM((2, 512, 128), F32),
            blocks(4, 8), blocks(8, 4),
            blocks(8, 8), blocks(8, 4),
            blocks(8), blocks(4), blocks(8),
            dma((6,)),
        ] + [dma] * 24,
        compiler_params=pltpu.CompilerParams(
            collective_id=0, has_side_effects=True, vmem_limit_bytes=20 * 1024 * 1024
        ),
        name="cross_attention",
    )(*(
        pltpu.with_memory_space_constraint(a, pltpu.HBM)
        for a in (
            vision_states,
            projection.reshape(2048, 128),
            queries.reshape(TOK, HEAD_DIM),
            cotangent.reshape(TOK, HEAD_DIM),
            gate_logit,
            tile_counts,
        )
    ))
    return (
        attended.reshape(queries.shape),
        query_grad.reshape(queries.shape),
        image_grad,
    )


def solution(mesh):
    return jax.shard_map(
        on_device,
        mesh=mesh,
        in_specs=(
            P("section", "tensor"),
            P("section", "tensor", None, None, None),
            P("section", None, "tensor"),
            P("section", None, "tensor"),
            P(),
            P(),
        ),
        out_specs=(
            P("section", None, "tensor"),
            P("section", None, "tensor"),
            P("section", "tensor"),
        ),
        check_vma=False,
    )
```

time: 74.6 us -> 69.6 us (0.933)
  Pallas kernels: 70.4 us -> 66 us
  local copies, waits for them, and re-layouts: 3.33 us -> 2.19 us
    pallas_call x1, Pallas kernels: 70.4 us -> 66 us  [on_device(): pl.pallas_call(kernel, out_shape=(jax.ShapeDtypeStruct((TOK, HEAD_DIM), B...]
    unnamed x7 -> x3, local copies, waits for them, and re-layouts: 3.33 us -> 2.19 us
where the time goes in v2:
time: 69.6 us; the launch traced here: 68.8 us
  Pallas kernels  66 us (95%)
  local copies, waits for them, and re-layouts  2.19 us (3%)
    pallas_call x1, Pallas kernels, on_device(): pl.pallas_call(kernel, out_shape=(jax.ShapeDtypeStruct((TOK, HEAD_DIM), B...  66 us
    unnamed x3, local copies, waits for them, and re-layouts  2.19 us

profile of v2, /device:TPU:1, one launch (start us, length us, event | category | flops | bytes accessed | tf_op | source)
XLA Modules:
  0.0 68.8 jit_solution(15350869556710016295)
XLA Ops:
  0.6 66.0 %cross_attention.1 = (bf16[2048,128]{1,0:T(8,128)(2,1)S(1)}, bf16[2048,128]{1,0:T(8,128)(2,1)S(1)}, f32[4,512]{1,0:T(4,128)S(1)}) custom-call(bf16[4,512]{1,0:T(4,128)(2,1)} %vis_ref.1, bf16[2048,128]{1,0:T(8,128)(2,1)} %bitcast.7, bf16[2048,128]{1,0:T(8,128)(2,1)} %bitcast.8, bf16[2048,128]{1,0:T(8,128)(2,1)} %bitcast.9, f32[16]{0:T(128)} %gate_ref.1, ...), custom_call_target="tpu_custom_call" | custom-call | tf_op jit(solution)/shard_map/cross_attention/pallas_call | solution.py:381
  66.6 0.8 %copy.12 = bf16[1,2048,128]{2,1,0:T(8,128)(2,1)} copy(bf16[1,2048,128]{2,1,0:T(8,128)(2,1)S(1)} %bitcast.6) | data formatting | bytes 1048576
  67.4 0.8 %copy.13 = bf16[1,2048,128]{2,1,0:T(8,128)(2,1)} copy(bf16[1,2048,128]{2,1,0:T(8,128)(2,1)S(1)} %bitcast.5) | data formatting | bytes 1048576
  68.2 0.6 copy.14

commit v3 on v2

--- a/solution.py
+++ b/solution.py
@@ -30,10 +30,10 @@
     att_ref, qg_ref, img_ref,
     gate_s, count_s, vis_v, msg_f, msg, vin_a, vin_b, vf, vb_a, vb_b, w_raw, w_f, w_cat, w_t,
     q_v, cot_v, gi_v, q_t, gi_t, probs_s, ds_s,
-    part, r1, kv, grads, r2, r3, g_f, em_a, em_b, ea1, eb1, es_a, es_b, e2,
+    part, r1, kv, grads, r2, r3, g_f, e_msg, r4,
     load_sem, w_send, w_recv, a1_send, a1a_recv, a1b_recv, a2a_send, a2b_send, a2a_recv, a2b_recv,
     b1_send, b1_recv, b2_send, b2_recv, d1_send, d1_recv, d2_send, d2_recv,
-    ea1_send, eb1_send, ea1_recv, eb1_recv, e2a_send, e2b_send, e2_recv,
+    e_send, e_recv, ready,
 ):
     sec = lax.axis_index("section")
     ten = lax.axis_index("tensor")
@@ -80,17 +80,22 @@
         for c in range(2):
             greet(chip((x + d) % SIDE, y, c))
             greet(chip(x, (y + d) % SIDE, c))
-    for i in range(1, 8):
-        greet(tensor_peer(half * 8 + (slot + i) % 8))
-    for i in range(4):
-        greet(tensor_peer(((1 - half) * 4 + i) * 2 + core))
+    for i in range(8):
+        @pl.when(jnp.logical_and(i // 2 >= sum_tile, i != slot))
+        def _():
+            greet(tensor_peer(half * 8 + i))
+
+    @pl.when(half == 0)
+    def _():
+        for i in range(4):
+            greet(tensor_peer((4 + i) * 2 + core))
 
     load_v.wait()
     for k in range(4):
         msg_f[4 * k : 4 * k + 4, :] = vis_v[:, 128 * k : 128 * (k + 1)].astype(F32)
     msg[...] = msg_f[...].astype(BF16)
 
-    pl.semaphore_wait(barrier, 39)
+    pl.semaphore_wait(barrier, 29 + 2 * sum_tile + 4 * half)
 
     @pl.when(core == 0)
     def _():
@@ -118,8 +123,19 @@
         def _():
             remote(msg, vin_b.at[y, tile], a1_send, a1b_recv, chip(x, y, 0)).start()
 
-    w_copy = remote(w_ref, w_raw.at[core], w_send, w_recv, tensor_peer(z * 2 + 1 - core))
-    w_copy.start()
+    for i in range(6):
+        @pl.when(i // 2 < sum_tile)
+        def _():
+            pl.semaphore_signal(
+                ready, inc=1, device_id=tensor_peer(half * 8 + i), device_id_type=MESH
+            )
+
+    @pl.when(half == 1)
+    def _():
+        for i in range(4):
+            pl.semaphore_signal(
+                ready, inc=1, device_id=tensor_peer(i * 2 + core), device_id_type=MESH
+            )
 
     def lay_out(m):
         w_f[...] = w_raw[m].astype(F32)
@@ -141,6 +157,8 @@
         for d in FAR_FIRST:
             remote(vin_a.at[tile], vin_a.at[tile], a2a_send, a2a_recv, chip((x + d) % SIDE, y, core)).start()
 
+    w_copy = remote(w_ref, w_raw.at[core], w_send, w_recv, tensor_peer(z * 2 + 1 - core))
+    w_copy.start()
     load_g.wait()
     load_n.wait()
     gate = jnp.tanh(jnp.full((8, 128), gate_s[sec // GROUPS], F32))[0:1, 0:1]
@@ -181,6 +199,11 @@
     )
     for g in range(2):
         part[4 * g : 4 * g + 4] = total[:, 256 * g : 256 * (g + 1)].reshape(4, 32, 256)
+
+    @pl.when(z < SIDE - 1)
+    def _():
+        pl.semaphore_wait(ready, 2 * (3 - sum_tile) + 4 * (1 - half))
+
     for d in FAR_FIRST:
         dest = (z + d) % 8
         remote(part.at[dest], r1.at[z], b1_send, b1_recv, tensor_peer(dest * 2 + core)).start()
@@ -258,64 +281,35 @@
     arrived(r3.at[pl.ds(0, 7)], d2_recv)
 
     sums = jnp.concatenate([r3[0:4].reshape(128, 256), r3[4:8].reshape(128, 256)], axis=1)
-
-    def spread(m, where, step):
+    for m in range(2):
         grad = jnp.dot(sums, w_t[m], preferred_element_type=F32)
         for j in range(TILES):
             for k in range(4):
                 for r in range(4):
-                    g_f[m, pl.ds(where(j) + 4 * k + r, 8, stride=step), :] = grad[
+                    g_f[pl.ds(256 * j + 16 * m + 4 * k + r, 8, stride=32), :] = grad[
                         32 * j + 8 * r : 32 * j + 8 * (r + 1), 128 * k : 128 * (k + 1)
                     ]
-        return g_f[m].astype(BF16)
-
-    em_b[...] = spread(1, lambda j: 16 * j, 64).reshape(8, 4, 16, 128)
-    for d in FAR_FIRST:
-        ty = (y + d) % SIDE
-        remote(em_b.at[ty], eb1.at[y], eb1_send, eb1_recv, chip(x, ty, core)).start()
-    em_a[...] = spread(0, lambda j: 128 * j, 16).reshape(4, 8, 16, 128)
-    own_a = jnp.logical_and(core == 0, is_own)
-    own_b = jnp.logical_and(core == 1, is_own)
+    e_msg[...] = g_f[...].astype(BF16).reshape(4, 8, 2, 16, 128)
     for i in range(4):
         j = (tile + 2 + i) % 4
-        me = jnp.logical_and(own_a, j == tile)
-
-        @pl.when(me)
-        def _():
-            pltpu.make_async_copy(em_a.at[j], ea1.at[x], ea1_recv).start()
-
-        @pl.when(jnp.logical_not(me))
-        def _():
-            remote(em_a.at[j], ea1.at[x], ea1_send, ea1_recv, chip(4 * core + j, y, 0)).start()
-
-    arrived(eb1.at[pl.ds(0, 7)], eb1_recv)
-    total = em_b[y].astype(F32)
-    for d in range(1, 8):
-        total = total + eb1[(y + d) % 8].astype(F32)
-    es_b[...] = total.astype(BF16)
-    for i in range(4):
-        j = (tile + 2 + i) % 4
-        me = jnp.logical_and(own_b, j == tile)
-
-        @pl.when(me)
-        def _():
-            pltpu.make_async_copy(es_b.at[j], e2.at[x], e2_recv).start()
-
-        @pl.when(jnp.logical_not(me))
-        def _():
-            remote(es_b.at[j], e2.at[x], e2b_send, e2_recv, chip(4 * core + j, y, 1)).start()
-
-    @pl.when(core == 0)
-    def _():
-        arrived(ea1, ea1_recv)
-        total = ea1[0].astype(F32)
-        for i in range(1, 8):
-            total = total + ea1[i].astype(F32)
-        es_a[...] = total.astype(BF16)
         for d in FAR_FIRST:
             ty = (y + d) % SIDE
-            remote(es_a.at[ty], e2.at[y], e2a_send, e2_recv, chip(x, ty, 0)).start()
-        e2[y] = es_a[y]
+            for m in range(2):
+                remote(
+                    e_msg.at[j, ty, m], r4.at[sec], e_send, e_recv, chip(4 * core + j, ty, m)
+                ).start()
+        for m in range(2):
+            me = jnp.logical_and(is_own, jnp.logical_and(j == tile, core == m))
+
+            @pl.when(me)
+            def _():
+                pltpu.make_async_copy(e_msg.at[j, y, m], r4.at[sec], e_recv).start()
+
+            @pl.when(jnp.logical_not(me))
+            def _():
+                remote(
+                    e_msg.at[j, y, m], r4.at[sec], e_send, e_recv, chip(4 * core + j, y, m)
+                ).start()
 
     w_copy.wait_send()
     arrived(vin_b.at[pl.ds(0, 7)], a2b_send)
@@ -323,48 +317,34 @@
     arrived(kv.at[pl.ds(0, 7)], b2_send)
     arrived(grads.at[pl.ds(0, 7)], d1_send)
     arrived(r3.at[pl.ds(0, 7)], d2_send)
-    arrived(em_b.at[pl.ds(0, 7)], eb1_send)
 
     @pl.when(is_own)
     def _():
         arrived(vin_a.at[0, pl.ds(0, 7)], a1_send)
-        arrived(ea1.at[pl.ds(0, 7)], a2a_send)
+        arrived(r4.at[pl.ds(0, 56)], a2a_send)
+        arrived(r4.at[pl.ds(0, 63)], e_send)
 
     @pl.when(jnp.logical_not(is_own))
     def _():
         arrived(vin_a.at[0], a1_send)
-
-    @pl.when(own_a)
-    def _():
-        arrived(em_a.at[pl.ds(0, 3)], ea1_send)
-
-    @pl.when(jnp.logical_not(own_a))
-    def _():
-        arrived(em_a, ea1_send)
-
-    @pl.when(own_b)
-    def _():
-        arrived(es_b.at[pl.ds(0, 3)], e2b_send)
-
-    @pl.when(jnp.logical_not(own_b))
-    def _():
-        arrived(es_b, e2b_send)
-
-    @pl.when(core == 0)
-    def _():
-        arrived(es_a.at[pl.ds(0, 7)], e2a_send)
-
-    @pl.when(core == 0)
-    def _():
-        arrived(e2.at[pl.ds(0, 7)], e2_recv)
-
-    @pl.when(core == 1)
-    def _():
-        arrived(e2, e2_recv)
-
-    image = jnp.sum(e2[...].astype(F32), axis=0)
+        arrived(r4, e_send)
+
+    arrived(r4, e_recv)
+    image = jnp.sum(r4[...].astype(F32), axis=0)
     for k in range(4):
         img_ref[:, 128 * k : 128 * (k + 1)] = image[4 * k : 4 * k + 4, :]
+
+
+def copy_out(att_v, qg_v, img_v, att_ref, qg_ref, img_ref, sem):
+    copies = [pltpu.make_async_copy(img_v, img_ref, sem.at[8])]
+    for i in range(4):
+        rows = pl.ds(i * (TOK // 4), TOK // 4)
+        copies.append(pltpu.make_async_copy(att_v.at[rows], att_ref.at[rows], sem.at[i]))
+        copies.append(pltpu.make_async_copy(qg_v.at[rows], qg_ref.at[rows], sem.at[4 + i]))
+    for copy in copies:
+        copy.start()
+    for copy in copies:
+        copy.wait()
 
 
 def on_device(vision_states, projection, queries, cotangent, gate_logit, tile_counts):
@@ -405,12 +385,10 @@
             pltpu.VMEM((8, 32, 256), F32),
             pltpu.VMEM((8, 32, 256), F32),
             tile8, tile8, tile8, tile8,
-            pltpu.VMEM((2, 512, 128), F32),
-            blocks(4, 8), blocks(8, 4),
-            blocks(8, 8), blocks(8, 4),
-            blocks(8), blocks(4), blocks(8),
+            pltpu.VMEM((1024, 128), F32),
+            blocks(4, 8, 2), blocks(64),
             dma((6,)),
-        ] + [dma] * 24,
+        ] + [dma] * 19 + [pltpu.SemaphoreType.REGULAR],
         compiler_params=pltpu.CompilerParams(
             collective_id=0, has_side_effects=True, vmem_limit_bytes=20 * 1024 * 1024
         ),
@@ -426,6 +404,16 @@
             tile_counts,
         )
     ))
+    results = (attended, query_grad, image_grad)
+    attended, query_grad, image_grad = pl.pallas_call(
+        copy_out,
+        out_shape=tuple(jax.ShapeDtypeStruct(a.shape, a.dtype) for a in results),
+        in_specs=[pl.BlockSpec(memory_space=pl.ANY)] * 3,
+        out_specs=(hbm,) * 3,
+        scratch_shapes=[dma((9,))],
+        compiler_params=pltpu.CompilerParams(vmem_limit_bytes=1024 * 1024),
+        name="copy_out",
+    )(*results)
     return (
         attended.reshape(queries.shape),
         query_grad.reshape(queries.shape),

time: 69.6 us -> 67.3 us (0.967)
  local copies, waits for them, and re-layouts: 2.19 us -> 0 us
    unnamed x3 -> x0, local copies, waits for them, and re-layouts: 2.19 us -> none
    pallas_call x1, Pallas kernels: 66 us -> 64.7 us  [on_device(): pl.pallas_call(kernel, out_shape=(jax.ShapeDtypeStruct((TOK, HEAD_DIM), B...]
    pallas_call x0 -> x1, Pallas kernels: none -> 1.04 us  [on_device(): pl.pallas_call(copy_out, out_shape=tuple((jax.ShapeDtypeStruct(a.shape, a...]
where the time goes in v3:
time: 67.3 us; the launch traced here: 66.4 us
  Pallas kernels  65.8 us (98%)
    pallas_call x1, Pallas kernels, on_device(): pl.pallas_call(kernel, out_shape=(jax.ShapeDtypeStruct((TOK, HEAD_DIM), B...  64.7 us

profile of v3, /device:TPU:1, one launch (start us, length us, event | category | flops | bytes accessed | tf_op | source)
XLA Modules:
  0.0 66.4 jit_solution(18097532820746804713)
XLA Ops:
  0.6 64.7 %cross_attention.1 = (bf16[2048,128]{1,0:T(8,128)(2,1)S(1)}, bf16[2048,128]{1,0:T(8,128)(2,1)S(1)}, f32[4,512]{1,0:T(4,128)S(1)}) custom-call(bf16[4,512]{1,0:T(4,128)(2,1)} %vis_ref.1, bf16[2048,128]{1,0:T(8,128)(2,1)} %bitcast.5, bf16[2048,128]{1,0:T(8,128)(2,1)} %bitcast.6, bf16[2048,128]{1,0:T(8,128)(2,1)} %bitcast.7, f32[16]{0:T(128)} %gate_ref.1, ...), custom_call_target="tpu_custom_call" | custom-call | tf_op jit(solution)/shard_map/cross_attention/pallas_call | solution.py:361
  65.4 1.0 %copy_out.1 = (bf16[2048,128]{1,0:T(8,128)(2,1)}, bf16[2048,128]{1,0:T(8,128)(2,1)}, f32[4,512]{1,0:T(4,128)}) custom-call(bf16[2048,128]{1,0:T(8,128)(2,1)S(1)} %get-tuple-element.9.att_v, bf16[2048,128]{1,0:T(8,128)(2,1)S(1)} %get-tuple-element.10.qg_v, f32[4,512]{1,0:T(4,128)S(1)} %get-tuple-element.11.img_v), custom_call_target="tpu_custom_call" | custom-call | tf_op jit(solution)/shard_map/copy_out/pallas_call | solution.py:408

commit v4 on v3

--- a/solution.py
+++ b/solution.py
@@ -275,41 +275,61 @@
 
     for d in FAR_FIRST:
         remote(
-            r3.at[z], r3.at[z], d2_send, d2_recv, tensor_peer(((z + d) % 8) * 2 + core)
+            r3.at[z], r3.at[z], d2_send, d2_recv.at[int(d != 4)],
+            tensor_peer(((z + d) % 8) * 2 + core),
         ).start()
     outputs(1)
-    arrived(r3.at[pl.ds(0, 7)], d2_recv)
-
-    sums = jnp.concatenate([r3[0:4].reshape(128, 256), r3[4:8].reshape(128, 256)], axis=1)
-    for m in range(2):
-        grad = jnp.dot(sums, w_t[m], preferred_element_type=F32)
-        for j in range(TILES):
-            for k in range(4):
-                for r in range(4):
-                    g_f[pl.ds(256 * j + 16 * m + 4 * k + r, 8, stride=32), :] = grad[
-                        32 * j + 8 * r : 32 * j + 8 * (r + 1), 128 * k : 128 * (k + 1)
-                    ]
-    e_msg[...] = g_f[...].astype(BF16).reshape(4, 8, 2, 16, 128)
-    for i in range(4):
-        j = (tile + 2 + i) % 4
+    def image_rows(steps):
+        count = len(steps)
+        places = [(sum_tile + step) % 4 for step in steps]
+        sums = jnp.concatenate(
+            [
+                jnp.concatenate([r3[place] for place in places], axis=0),
+                jnp.concatenate([r3[4 + place] for place in places], axis=0),
+            ],
+            axis=1,
+        )
+        for m in range(2):
+            grad = jnp.dot(sums, w_t[m], preferred_element_type=F32)
+            for j in range(count):
+                for k in range(4):
+                    for r in range(4):
+                        g_f[pl.ds(256 * steps[j] + 16 * m + 4 * k + r, 8, stride=32), :] = grad[
+                            32 * j + 8 * r : 32 * j + 8 * (r + 1), 128 * k : 128 * (k + 1)
+                        ]
+        low = steps[0]
+        e_msg[low : low + count] = (
+            g_f[256 * low : 256 * (low + count), :].astype(BF16).reshape(count, 8, 2, 16, 128)
+        )
+
+    def send_rows(step):
+        j = (sum_tile + step) % 4
         for d in FAR_FIRST:
             ty = (y + d) % SIDE
             for m in range(2):
                 remote(
-                    e_msg.at[j, ty, m], r4.at[sec], e_send, e_recv, chip(4 * core + j, ty, m)
+                    e_msg.at[step, ty, m], r4.at[sec], e_send, e_recv, chip(4 * core + j, ty, m)
                 ).start()
         for m in range(2):
             me = jnp.logical_and(is_own, jnp.logical_and(j == tile, core == m))
 
             @pl.when(me)
             def _():
-                pltpu.make_async_copy(e_msg.at[j, y, m], r4.at[sec], e_recv).start()
+                pltpu.make_async_copy(e_msg.at[step, y, m], r4.at[sec], e_recv).start()
 
             @pl.when(jnp.logical_not(me))
             def _():
                 remote(
-                    e_msg.at[j, y, m], r4.at[sec], e_send, e_recv, chip(4 * core + j, y, m)
+                    e_msg.at[step, y, m], r4.at[sec], e_send, e_recv, chip(4 * core + j, y, m)
                 ).start()
+
+    arrived(r3.at[pl.ds(0, 6)], d2_recv.at[1])
+    image_rows((1, 2, 3))
+    for i in range(3):
+        send_rows(1 + (tile + i) % 3)
+    arrived(r3.at[0], d2_recv.at[0])
+    image_rows((0,))
+    send_rows(0)
 
     w_copy.wait_send()
     arrived(vin_b.at[pl.ds(0, 7)], a2b_send)
@@ -388,7 +408,7 @@
             pltpu.VMEM((1024, 128), F32),
             blocks(4, 8, 2), blocks(64),
             dma((6,)),
-        ] + [dma] * 19 + [pltpu.SemaphoreType.REGULAR],
+        ] + [dma] * 16 + [dma((2,))] + [dma] * 2 + [pltpu.SemaphoreType.REGULAR],
         compiler_params=pltpu.CompilerParams(
             collective_id=0, has_side_effects=True, vmem_limit_bytes=20 * 1024 * 1024
         ),

time: 67.3 us -> 67.5 us (level); the launches traced: 66.4 us -> 67.3 us
  Pallas kernels: 65.8 us -> 66.6 us
    pallas_call x1, Pallas kernels: 64.7 us -> 65.6 us  [on_device(): pl.pallas_call(kernel, out_shape=(jax.ShapeDtypeStruct((TOK, HEAD_DIM), B...]
where the time goes in v4:
time: 67.5 us; the launch traced here: 67.3 us
  Pallas kernels  66.6 us (99%)
    pallas_call x1, Pallas kernels, on_device(): pl.pallas_call(kernel, out_shape=(jax.ShapeDtypeStruct((TOK, HEAD_DIM), B...  65.6 us

profile of v4, /device:TPU:1, one launch (start us, length us, event | category | flops | bytes accessed | tf_op | source)
XLA Modules:
  0.0 67.3 jit_solution(14132992063541189711)
XLA Ops:
  0.6 65.6 %cross_attention.1 = (bf16[2048,128]{1,0:T(8,128)(2,1)S(1)}, bf16[2048,128]{1,0:T(8,128)(2,1)S(1)}, f32[4,512]{1,0:T(4,128)S(1)}) custom-call(bf16[4,512]{1,0:T(4,128)(2,1)} %vis_ref.1, bf16[2048,128]{1,0:T(8,128)(2,1)} %bitcast.5, bf16[2048,128]{1,0:T(8,128)(2,1)} %bitcast.6, bf16[2048,128]{1,0:T(8,128)(2,1)} %bitcast.7, f32[16]{0:T(128)} %gate_ref.1, ...), custom_call_target="tpu_custom_call" | custom-call | tf_op jit(solution)/shard_map/cross_attention/pallas_call | solution.py:381
  66.2 1.0 %copy_out.1 = (bf16[2048,128]{1,0:T(8,128)(2,1)}, bf16[2048,128]{1,0:T(8,128)(2,1)}, f32[4,512]{1,0:T(4,128)}) custom-call(bf16[2048,128]{1,0:T(8,128)(2,1)S(1)} %get-tuple-element.9.att_v, bf16[2048,128]{1,0:T(8,128)(2,1)S(1)} %get-tuple-element.10.qg_v, f32[4,512]{1,0:T(4,128)S(1)} %get-tuple-element.11.img_v), custom_call_target="tpu_custom_call" | custom-call | tf_op jit(solution)/shard_map/copy_out/pallas_call | solution.py:428
